TPU v7x, 32 devices: a whole 2x2x4 slice. The times are simulated.
32 devices in a mesh: dp: 4 (over x, core), fsdp: 8 (over z, y).
Axes of the slice: x: 2, y: 2, z: 4, core: 2. Of those that a mesh axis runs over, the one named last changes fastest.
Arguments:
- mel_clips: bfloat16 [640, 256, 512], P(('dp', 'fsdp')), may hold values from -6 to 6
- live_counts: int32 [32, 4], P(('dp', 'fsdp')), may hold values from 1 to 5, as said below
- conv_weight: bfloat16 [512, 7], P(('dp', 'fsdp')), may hold values from -2 to 2
- conv_bias: bfloat16 [512], P(('dp', 'fsdp')), may hold values from -3 to 3
- norm_gain: bfloat16 [512], P(('dp', 'fsdp')), may hold values from 0.25 to 1.75
- norm_shift: bfloat16 [512], P(('dp', 'fsdp')), may hold values from -2 to 2
- in_weight: bfloat16 [512, 1536], P(('dp', 'fsdp')), may hold values from -0.25 to 0.25
- in_bias: bfloat16 [1536], P(('dp', 'fsdp')), may hold values from -2 to 2
- out_weight: bfloat16 [1536, 512], P(('dp', 'fsdp')), may hold values from -0.3125 to 0.3125
- out_bias: bfloat16 [512], P(('dp', 'fsdp')), may hold values from -2 to 2
- layer_scale: bfloat16 [512], P(('dp', 'fsdp')), may hold values from 0.29882812 to 1.1953125
- cotangent: bfloat16 [640, 256, 512], P(('dp', 'fsdp')), may hold values from -6 to 6
Outputs:
- block_out: bfloat16 [640, 256, 512], P(('dp', 'fsdp'))
- grad_clips: bfloat16 [640, 256, 512], P(('dp', 'fsdp'))
- grad_conv_weight: float32 [512, 7], P(('dp', 'fsdp'))
- grad_conv_bias: float32 [512], P(('dp', 'fsdp'))
- grad_norm_gain: float32 [512], P(('dp', 'fsdp'))
- grad_norm_shift: float32 [512], P(('dp', 'fsdp'))
- grad_in_weight: float32 [512, 1536], P(('dp', 'fsdp'))
- grad_in_bias: float32 [1536], P(('dp', 'fsdp'))
- grad_out_weight: float32 [1536, 512], P(('dp', 'fsdp'))
- grad_out_bias: float32 [512], P(('dp', 'fsdp'))
- grad_layer_scale: float32 [512], P(('dp', 'fsdp'))
Inputs may be any that keep to these rules, and one draw needn't show every extreme that they name: Slot s of micro-batch m on device d holds a live clip when s < live_counts[d, m]; some device has all 5 slots live in some micro-batch, and some device only one.
All inputs are finite; a program needn't handle non-finite values.
Results may differ from a plain program's by a relative error of at most 0.0063.
Values may be sent and summed in bfloat16 or wider, within the bound.
A program may use at most 256 MiB of HBM per device.

v0:
```python
from functools import partial
import jax
import jax.numpy as jnp
from jax import lax
from jax.sharding import PartitionSpec as P


def conv_norm(mel_block, conv_weight, conv_bias, norm_gain, norm_shift):
    frames = mel_block.shape[1]
    kernel = conv_weight.shape[1]
    margin = (kernel - 1) // 2
    padded = jnp.pad(mel_block, ((0, 0), (margin, margin), (0, 0)))
    mixed_sum = conv_bias + padded[:, 0:frames, :] * conv_weight[:, 0]
    for offset in range(1, kernel):
        mixed_sum = mixed_sum + padded[:, offset : offset + frames, :] * conv_weight[:, offset]
    center = mixed_sum - jnp.mean(mixed_sum, axis=-1, keepdims=True)
    spread = jnp.mean(center * center, axis=-1, keepdims=True)
    return center * lax.rsqrt(spread + 1e-06) * norm_gain + norm_shift


def contract_rows(left_side, right_side):
    return lax.dot_general(
        left_side, right_side, (((0,), (0,)), ((), ())), preferred_element_type=jnp.float32
    )


def contract_last(left_side, right_side):
    return lax.dot_general(
        left_side, right_side, (((1,), (1,)), ((), ())), preferred_element_type=jnp.float32
    )


def on_device(
    mel_clips,
    live_counts,
    conv_weight,
    conv_bias,
    norm_gain,
    norm_shift,
    in_weight,
    in_bias,
    out_weight,
    out_bias,
    layer_scale,
    cotangent,
):
    shards = (
        conv_weight,
        conv_bias,
        norm_gain,
        norm_shift,
        in_weight,
        in_bias,
        out_weight,
        out_bias,
        layer_scale,
    )
    micro_count = live_counts.shape[1]
    slot_count = mel_clips.shape[0] // micro_count
    channels = mel_clips.shape[2]
    devices = lax.axis_size(("dp", "fsdp"))
    totals = tuple(
        (jnp.zeros((piece.shape[0] * devices,) + piece.shape[1:], jnp.float32) for piece in shards)
    )
    block_outs = []
    block_grads = []
    for micro_step in range(micro_count):
        forward_set = (
            lax.all_gather(conv_weight, ("dp", "fsdp"), axis=0, tiled=True),
            lax.all_gather(conv_bias, ("dp", "fsdp"), axis=0, tiled=True),
            lax.all_gather(norm_gain, ("dp", "fsdp"), axis=0, tiled=True),
            lax.all_gather(norm_shift, ("dp", "fsdp"), axis=0, tiled=True),
            lax.all_gather(in_weight, ("dp", "fsdp"), axis=0, tiled=True),
            lax.all_gather(in_bias, ("dp", "fsdp"), axis=0, tiled=True),
            lax.all_gather(out_weight, ("dp", "fsdp"), axis=0, tiled=True),
            lax.all_gather(out_bias, ("dp", "fsdp"), axis=0, tiled=True),
            lax.all_gather(layer_scale, ("dp", "fsdp"), axis=0, tiled=True),
        )
        (
            full_conv,
            full_cbias,
            full_gain,
            full_shift,
            full_in,
            full_ibias,
            full_out,
            full_obias,
            full_scale,
        ) = forward_set
        clip_block = mel_clips[micro_step * slot_count : (micro_step + 1) * slot_count].astype(
            jnp.float32
        )
        live_mask = (lax.iota(jnp.int32, slot_count) < live_counts[0, micro_step]).astype(
            jnp.float32
        )
        normed, norm_pull = jax.vjp(
            conv_norm,
            clip_block,
            full_conv.astype(jnp.float32),
            full_cbias.astype(jnp.float32),
            full_gain.astype(jnp.float32),
            full_shift.astype(jnp.float32),
        )
        rows_low = normed.reshape(-1, channels).astype(jnp.bfloat16)
        hidden = jnp.dot(rows_low, full_in, preferred_element_type=jnp.float32) + full_ibias.astype(
            jnp.float32
        )
        active, gelu_pull = jax.vjp(partial(jax.nn.gelu, approximate=False), hidden)
        active_low = active.astype(jnp.bfloat16)
        output = jnp.dot(
            active_low, full_out, preferred_element_type=jnp.float32
        ) + full_obias.astype(jnp.float32)
        output = output.reshape(clip_block.shape)
        scale_full = full_scale.astype(jnp.float32)
        branch = output * scale_full * live_mask[:, None, None]
        block_outs.append((clip_block + branch).astype(jnp.bfloat16))
        back_in, back_out, scale_back = (
            lax.all_gather(in_weight, ("dp", "fsdp"), axis=0, tiled=True),
            lax.all_gather(out_weight, ("dp", "fsdp"), axis=0, tiled=True),
            lax.all_gather(layer_scale, ("dp", "fsdp"), axis=0, tiled=True),
        )
        back_scale = scale_back.astype(jnp.float32)
        grad_out = cotangent[micro_step * slot_count : (micro_step + 1) * slot_count].astype(
            jnp.float32
        )
        masked_out = grad_out * live_mask[:, None, None]
        grad_scale = jnp.sum((masked_out * output).reshape(-1, channels), axis=0)
        grad_output = (masked_out * back_scale).reshape(-1, channels).astype(jnp.bfloat16)
        grad_obias = jnp.sum(grad_output.astype(jnp.float32), axis=0)
        grad_wout = contract_rows(active_low, grad_output)
        grad_active = contract_last(grad_output, back_out)
        (grad_hidden,) = gelu_pull(grad_active)
        hidden_low = grad_hidden.astype(jnp.bfloat16)
        grad_ibias = jnp.sum(hidden_low.astype(jnp.float32), axis=0)
        grad_win = contract_rows(rows_low, hidden_low)
        grad_normed = contract_last(hidden_low, back_in)
        grad_input, grad_conv, grad_cbias, grad_gain, grad_shift = norm_pull(
            grad_normed.reshape(clip_block.shape)
        )
        block_grads.append((grad_out + grad_input).astype(jnp.bfloat16))
        parts_now = (
            grad_conv,
            grad_cbias,
            grad_gain,
            grad_shift,
            grad_win,
            grad_ibias,
            grad_wout,
            grad_obias,
            grad_scale,
        )
        totals = tuple((a + b for a, b in zip(totals, parts_now)))
    grad_sums = (
        lax.psum_scatter(totals[0], ("dp", "fsdp"), scatter_dimension=0, tiled=True),
        lax.psum_scatter(totals[1], ("dp", "fsdp"), scatter_dimension=0, tiled=True),
        lax.psum_scatter(totals[2], ("dp", "fsdp"), scatter_dimension=0, tiled=True),
        lax.psum_scatter(totals[3], ("dp", "fsdp"), scatter_dimension=0, tiled=True),
        lax.psum_scatter(totals[4], ("dp", "fsdp"), scatter_dimension=0, tiled=True),
        lax.psum_scatter(totals[5], ("dp", "fsdp"), scatter_dimension=0, tiled=True),
        lax.psum_scatter(totals[6], ("dp", "fsdp"), scatter_dimension=0, tiled=True),
        lax.psum_scatter(totals[7], ("dp", "fsdp"), scatter_dimension=0, tiled=True),
        lax.psum_scatter(totals[8], ("dp", "fsdp"), scatter_dimension=0, tiled=True),
    )
    block_out = jnp.concatenate(block_outs, axis=0)
    grad_clips = jnp.concatenate(block_grads, axis=0)
    return (
        block_out,
        grad_clips,
        grad_sums[0],
        grad_sums[1],
        grad_sums[2],
        grad_sums[3],
        grad_sums[4],
        grad_sums[5],
        grad_sums[6],
        grad_sums[7],
        grad_sums[8],
    )


def solution(mesh):
    in_specs = (
        P(("dp", "fsdp"), None, None),
        P(("dp", "fsdp"), None),
        P(("dp", "fsdp"), None),
        P(("dp", "fsdp")),
        P(("dp", "fsdp")),
        P(("dp", "fsdp")),
        P(("dp", "fsdp"), None),
        P(("dp", "fsdp")),
        P(("dp", "fsdp"), None),
        P(("dp", "fsdp")),
        P(("dp", "fsdp")),
        P(("dp", "fsdp"), None, None),
    )
    out_specs = (
        P(("dp", "fsdp"), None, None),
        P(("dp", "fsdp"), None, None),
        P(("dp", "fsdp"), None),
        P(("dp", "fsdp")),
        P(("dp", "fsdp")),
        P(("dp", "fsdp")),
        P(("dp", "fsdp"), None),
        P(("dp", "fsdp")),
        P(("dp", "fsdp"), None),
        P(("dp", "fsdp")),
        P(("dp", "fsdp")),
    )
    return jax.shard_map(
        on_device, mesh=mesh, in_specs=in_specs, out_specs=out_specs, check_vma=False
    )
```

profile of v0, /device:TPU:0, one launch (start us, length us, event | category | flops | bytes accessed | tf_op | source)
XLA Modules:
  0.0 748.3 jit_solution(5183348924312344757)
XLA Ops:
  13.8 42.2 %all-reduce.73 = (bf16[512]{0:T(512)(128)(2,1)S(1)}, bf16[512]{0:T(512)(128)(2,1)S(1)}, bf16[512]{0:T(512)(128)(2,1)S(1)}, bf16[1536]{0:T(1024)(128)(2,1)S(1)}, ...) all-reduce(bf16[512]{0:T(512)(128)(2,1)S(1)} %dynamic-update-slice,, ...), channel_id=1, replica_groups=mesh['dp'=4,'fsdp'=8] {'dp','fsdp'}, use_global_device_ids=true, to_apply=%add.60 | all-reduce | flops 4096 | bytes 16384
  56.0 66.8 %all-gather = bf16[32,16,7]{1,2,0:T(8,128)(2,1)S(1)} all-gather(bf16[1,16,7]{1,2,0:T(8,128)(2,1)} %bitcast.200), channel_id=1, replica_groups=mesh['dp'=4,'fsdp'=8] {'dp','fsdp'}, dimensions={0}, use_global_device_ids=true | all-gather | bytes 7392 | tf_op jit(solution)/shard_map/all_gather | solution.py:69
  123.2 7.1 slice_convert_fusion.3
  130.4 28.4 %fusion.61 = (f32[5,256]{1,0:T(8,128)S(1)}, f32[5,256,512]{2,1,0:T(8,128)S(1)}, f32[5,256]{1,0:T(8,128)S(1)}, f32[5,256,512]{2,1,0:T(8,128)S(1)}, f32[5,256]{1,0...) fusion(f32[512]{0:T(512)S(1)} %bitcast.152, f32[512]{0:T(512)S(1)} %bitcast.143, ...), kind=kLoop, calls=%fused_computation.295 | loop fusion | flops 39316480 | bytes 21008384 | tf_op jit(solution)/shard_map/jvp()/reduce_sum | solution.py:16
  163.9 1.8 compare_convert_fusion
  165.7 1.8 compare_convert_fusion.2
  167.6 3.7 add_convert_fusion.11
  171.3 22.9 %multiply_convert_fusion.2 = (bf16[1280,1536]{1,0:T(8,128)(2,1)}, f32[1280,1536]{1,0:T(8,128)}, f32[1280,1536]{1,0:T(8,128)}) fusion(f32[1536]{0:T(1024)S(1)} %convert_element_type.238, bf16[1280,512]{1,0:T(8,128)(2,1)} %bitcast.129, bf16[512,1536]{1,0:T(8,128)(2,1)} %all-gather.4.cloned.1.call-done), kind=kOutput, calls=%fused_computation.46 | convolution fusion | flops 2143027200 | bytes 22550528 | tf_op jit(solution)/shard_map/dot_general | solution.py:105
  194.2 20.9 %multiply_convert_fusion = (bf16[1280,1536]{1,0:T(8,128)(2,1)}, f32[1280,1536]{1,0:T(8,128)}, f32[1280,1536]{1,0:T(8,128)}) fusion(f32[1536]{0:T(1024)S(1)} %convert_element_type.238, bf16[1280,512]{1,0:T(8,128)(2,1)S(1)} %bitcast.125, bf16[512,1536]{1,0:T(8,128)(2,1)S(1)} %copy-done.86), kind=kOutput, calls=%fused_computation.20 | convolution fusion | flops 2143027200 | bytes 22550528 | tf_op jit(solution)/shard_map/dot_general | solution.py:105
  215.1 4.9 convolution_add_fusion.6
  220.1 2.2 convolution_add_fusion.4
  222.3 20.4 %multiply_convert_fusion.3 = (bf16[1280,1536]{1,0:T(8,128)(2,1)S(1)}, f32[1280,1536]{1,0:T(8,128)}, f32[1280,1536]{1,0:T(8,128)}) fusion(f32[1536]{0:T(1024)S(1)} %convert_element_type.238, bf16[1280,512]{1,0:T(8,128)(2,1)S(1)} %bitcast.133, bf16[512,1536]{1,0:T(8,128)(2,1)S(1)} %copy-done.86), kind=kOutput, calls=%fused_computation.59 | convolution fusion | flops 2143027200 | bytes 22550528 | tf_op jit(solution)/shard_map/dot_general | solution.py:105
  242.7 2.2 convolution_add_fusion.7
  245.0 20.4 %multiply_convert_fusion.1 = (bf16[1280,1536]{1,0:T(8,128)(2,1)S(1)}, f32[1280,1536]{1,0:T(8,128)}, f32[1280,1536]{1,0:T(8,128)}) fusion(f32[1536]{0:T(1024)S(1)} %convert_element_type.238, bf16[1280,512]{1,0:T(8,128)(2,1)S(1)} %bitcast.127, bf16[512,1536]{1,0:T(8,128)(2,1)S(1)} %copy-done.86), kind=kOutput, calls=%fused_computation.33 | convolution fusion | flops 2143027200 | bytes 22550528 | tf_op jit(solution)/shard_map/dot_general | solution.py:105
  265.4 2.2 convolution_add_fusion.5
  267.7 2.2 slice-done.2
  270.2 5.0 add_convert_fusion.10
  275.2 7.4 fusion.75
  282.7 7.8 %convert_reduce_fusion = (f32[1536]{0:T(1024)S(1)}, bf16[1280,1536]{1,0:T(8,128)(2,1)S(1)}) fusion(f32[1280,1536]{1,0:T(8,128)} %get-tuple-element.102, f32[1280,1536]{1,0:T(8,128)} %get-tuple-element.205, bf16[1280,512]{1,0:T(8,128)(2,1)S(1)} %bitcast.135, bf16[1536,512]{1,0:T(8,128)(2,1)S(1)} %copy-done.88), kind=kOutput, calls=%fused_computation.12 | convolution fusion | flops 2044721664 | bytes 22550528 | tf_op jit(solution)/shard_map/dot_general | solution.py:28
  290.5 2.2 fusion.70
  294.6 7.8 %convert_reduce_fusion.2 = (f32[1536]{0:T(1024)S(1)}, bf16[1280,1536]{1,0:T(8,128)(2,1)S(1)}) fusion(f32[1280,1536]{1,0:T(8,128)} %get-tuple-element.94, f32[1280,1536]{1,0:T(8,128)} %get-tuple-element.207, bf16[1280,512]{1,0:T(8,128)(2,1)S(1)} %bitcast.139, bf16[1536,512]{1,0:T(8,128)(2,1)S(1)} %copy-done.88), kind=kOutput, calls=%fused_computation.14 | convolution fusion | flops 2044721664 | bytes 22550528 | tf_op jit(solution)/shard_map/dot_general | solution.py:28
  302.4 2.2 fusion.73
  304.7 8.0 %convert_reduce_fusion.1 = (f32[1536]{0:T(1024)S(1)}, bf16[1280,1536]{1,0:T(8,128)(2,1)S(1)}) fusion(f32[1280,1536]{1,0:T(8,128)} %get-tuple-element.98, f32[1280,1536]{1,0:T(8,128)} %get-tuple-element.204, bf16[1280,512]{1,0:T(8,128)(2,1)S(1)} %bitcast.137, bf16[1536,512]{1,0:T(8,128)(2,1)S(1)} %copy-done.88), kind=kOutput, calls=%fused_computation.13 | convolution fusion | flops 2044721664 | bytes 22550528 | tf_op jit(solution)/shard_map/dot_general | solution.py:28
  312.7 2.2 fusion.71
  315.0 9.1 %convert_reduce_fusion.3 = (f32[1536]{0:T(1024)S(1)}, bf16[1280,1536]{1,0:T(8,128)(2,1)}) fusion(f32[1280,1536]{1,0:T(8,128)} %get-tuple-element.90, f32[1280,1536]{1,0:T(8,128)} %get-tuple-element.206, bf16[1280,512]{1,0:T(8,128)(2,1)S(1)} %bitcast.142, bf16[1536,512]{1,0:T(8,128)(2,1)S(1)} %copy-done.88), kind=kOutput, calls=%fused_computation.15 | convolution fusion | flops 2044721664 | bytes 22550528 | tf_op jit(solution)/shard_map/dot_general | solution.py:28
  324.1 4.6 fusion.72
  328.8 3.9 multiply_reduce_fusion.3
  332.9 4.4 fusion.56
  337.4 8.0 %multiply_reduce_fusion.31 = (f32[512]{0:T(512)S(1)}, f32[512]{0:T(512)S(1)}, f32[512]{0:T(512)S(1)}, f32[512]{0:T(512)S(1)}, f32[512]{0:T(512)S(1)}, /*index=5*...) fusion(f32[5,256,512]{2,1,0:T(8,128)S(1)} %copy-done.11, ...), kind=kLoop, calls=%fused_computation.179 | loop fusion | flops 13758976 | bytes 23626752 | tf_op jit(solution)/shard_map/transpose(jvp())/reduce_sum | solution.py:15
  345.4 19.1 %multiply_reduce_fusion.17 = (f32[512]{0:T(512)S(1)}, f32[512]{0:T(512)S(1)}, f32[512]{0:T(512)S(1)}, f32[512]{0:T(512)S(1)}, f32[512]{0:T(512)S(1)}, /*index=5*...) fusion(f32[5,256,512]{2,1,0:T(8,128)} %get-tuple-element.138, ...), kind=kLoop, calls=%fused_computation.165 | loop fusion | flops 17691648 | bytes 41979904 | tf_op jit(solution)/shard_map/transpose(jvp())/reduce_sum | solution.py:15
  364.5 15.1 %multiply_reduce_fusion.28 = (f32[512]{0:T(512)S(1)}, f32[512]{0:T(512)S(1)}, f32[512]{0:T(512)S(1)}, f32[512]{0:T(512)S(1)}, f32[512]{0:T(512)S(1)}, /*index=5*...) fusion(bf16[20,256,512]{2,1,0:T(8,128)(2,1)} %param.12, ...), kind=kLoop, calls=%fused_computation.176 | loop fusion | flops 20964864 | bytes 21020672 | tf_op jit(solution)/shard_map/transpose(jvp())/reduce_sum | solution.py:15
  379.7 8.0 %multiply_reduce_fusion.24 = (f32[512]{0:T(512)S(1)}, f32[512]{0:T(512)S(1)}, f32[512]{0:T(512)S(1)}, f32[512]{0:T(512)S(1)}, f32[512]{0:T(512)S(1)}, /*index=5*...) fusion(f32[5,256,512]{2,1,0:T(8,128)S(1)} %copy-done.10, ...), kind=kLoop, calls=%fused_computation.172 | loop fusion | flops 13104128 | bytes 23624704 | tf_op jit(solution)/shard_map/transpose(jvp())/reduce_sum | solution.py:15
  387.7 4.4 convolution_add_fusion.10
  392.2 4.0 convolution_add_fusion.9
  397.4 7.0 convolution_add_fusion.8
  405.7 4.6 fusion.74
  410.3 2.3 convolution_add_fusion.13
  412.8 2.2 convolution_add_fusion.12
  415.3 4.1 convolution_add_fusion.11
  419.5 37.4 %all-reduce.72 = (f32[512]{0:T(512)S(1)}, f32[512]{0:T(512)S(1)}, f32[512]{0:T(512)S(1)}, f32[1536]{0:T(1024)S(1)}, f32[512]{0:T(512)S(1)}, /*index=5*/f32[512]{0:T(512)S(1)}) all-reduce(f32[512]{0:T(512)S(1)} %add_add_fusion.10, f32[512]{0:T(512)S(1)} %add_add_fusion.9, ...), channel_id=3, replica_groups=mesh['dp'=4,'fsdp'=8] {'dp','fsdp'}, use_global_device_ids=true, to_apply=%region_49.50.clone | all-reduce | flops 4096 | bytes 32768
  460.4 5.3 add_convert_fusion.6
  465.7 15.9 %fusion.40 = (bf16[5,256,512]{2,1,0:T(8,128)(2,1)S(1)}, bf16[5,256,512]{2,1,0:T(8,128)(2,1)}) fusion(f32[5,256,512]{2,1,0:T(8,128)} %get-tuple-element.144, f32[5,256,512]{2,1,0:T(8,128)} %get-tuple-element.143, f32[5,256,512]{2,1,0:T(8,128)} %get-tuple-element.141, f32[5,256,512]{2,1,0:T(8,128)} %get-tuple-element.142, ...), kind=kLoop, calls=%fused_computation.116 | loop fusion | flops 11796480 | bytes 41943040 | tf_op jit(solution)/shard_map/convert_element_type | solution.py:140
  481.7 14.4 %fusion.41 = (bf16[5,256,512]{2,1,0:T(8,128)(2,1)}, bf16[5,256,512]{2,1,0:T(8,128)(2,1)}) fusion(f32[5,256,512]{2,1,0:T(8,128)} %get-tuple-element.151, f32[5,256,512]{2,1,0:T(8,128)} %get-tuple-element.150, f32[5,256,512]{2,1,0:T(8,128)} %get-tuple-element.148, f32[5,256,512]{2,1,0:T(8,128)} %get-tuple-element.149, f32[5,256,512]{2,1,0:T(8,128)} %get-tuple-element.146, ...), kind=kLoop, calls=%fused_computation.117 | loop fusion | flops 11796480 | bytes 41943040 | tf_op jit(solution)/shard_map/convert_element_type | solution.py:140
  496.1 6.4 pad_maximum_fusion.1
  502.5 3.0 pad_maximum_fusion
  505.5 24.7 %reduce-scatter.10.cloned.1.call-done = f32[16,7]{1,0:T(8,128)} async-done(((f32[512,7]{1,0:T(8,128)}), f32[16,7]{1,0:T(8,128)}) %reduce-scatter.10.cloned.1.call-update) | async-done | bytes 464
  531.5 103.0 %reduce-scatter.8.cloned.1.call-done = f32[48,512]{1,0:T(8,128)} async-done(((f32[1536,512]{1,0:T(8,128)}), f32[48,512]{1,0:T(8,128)}) %reduce-scatter.8.cloned.1.call-update) | async-done | bytes 98320 | tf_op jit(solution)/shard_map/reduce_scatter | solution.py:160
  634.5 107.0 %reduce-scatter.6.cloned.1.call-done = f32[16,1536]{1,0:T(8,128)} async-done(((f32[512,1536]{1,0:T(8,128)}), f32[16,1536]{1,0:T(8,128)}) %reduce-scatter.6.cloned.1.call-update) | async-done | bytes 98320 | tf_op jit(solution)/shard_map/reduce_scatter | solution.py:158
  (271 shorter events, 22.2 us)
Async XLA Ops:
  7.2 164.1 %all-gather.4.cloned.1.call-start = ((), (), s32[]{:S(2)}) async-start(), calls=%async_computation.3 | async-start | bytes 1622016 | tf_op jit(solution)/shard_map/all_gather | solution.py:73
  7.9 207.2 %all-gather.6.cloned.1.call-start = ((), (), s32[]{:S(2)}) async-start(), calls=%async_computation.4 | async-start | bytes 1622016 | tf_op jit(solution)/shard_map/all_gather | solution.py:75
  8.7 521.5 %reduce-scatter.10.cloned.1.call-start = ((), (), s32[]{:S(2)}) async-start(), calls=%async_computation.7 | async-start | bytes 270336
  123.1 7.2 copy-start.56
  123.1 7.2 copy-start.66
  123.2 7.2 copy-start.68
  123.2 7.2 copy-start.70
  123.2 7.2 copy-start.72
  123.2 7.2 copy-start.74
  123.2 7.2 copy-start.76
  158.7 8.8 %copy-start = (f32[5,256,512]{2,1,0:T(8,128)}, f32[5,256,512]{2,1,0:T(8,128)S(1)}, u32[]{:S(2)}) copy-start(f32[5,256,512]{2,1,0:T(8,128)S(1)} %get-tuple-element.92) | copy-start | bytes 7864324
  158.7 8.8 %copy-start.2 = (f32[5,256,512]{2,1,0:T(8,128)}, f32[5,256,512]{2,1,0:T(8,128)S(1)}, u32[]{:S(2)}) copy-start(f32[5,256,512]{2,1,0:T(8,128)S(1)} %get-tuple-element.168) | copy-start | bytes 7864324
  158.8 8.8 %copy-start.4 = (f32[5,256,512]{2,1,0:T(8,128)}, f32[5,256,512]{2,1,0:T(8,128)S(1)}, u32[]{:S(2)}) copy-start(f32[5,256,512]{2,1,0:T(8,128)S(1)} %get-tuple-element.170) | copy-start | bytes 7864324
  158.8 8.8 %copy-start.6 = (f32[5,256,512]{2,1,0:T(8,128)}, f32[5,256,512]{2,1,0:T(8,128)S(1)}, u32[]{:S(2)}) copy-start(f32[5,256,512]{2,1,0:T(8,128)S(1)} %get-tuple-element.172) | copy-start | bytes 7864324
  158.8 8.8 %copy-start.46 = (f32[5,256]{1,0:T(8,128)}, f32[5,256]{1,0:T(8,128)S(1)}, u32[]{:S(2)}) copy-start(f32[5,256]{1,0:T(8,128)S(1)} %broadcast_multiply_fusion.28) | copy-start | bytes 15364
  158.8 8.8 %copy-start.40 = (f32[5,256]{1,0:T(8,128)}, f32[5,256]{1,0:T(8,128)S(1)}, u32[]{:S(2)}) copy-start(f32[5,256]{1,0:T(8,128)S(1)} %broadcast_multiply_fusion.29) | copy-start | bytes 15364
  159.8 7.8 %copy-start.48 = (f32[5,256]{1,0:T(8,128)}, f32[5,256]{1,0:T(8,128)S(1)}, u32[]{:S(2)}) copy-start(f32[5,256]{1,0:T(8,128)S(1)} %fusion.50) | copy-start | bytes 15364
  160.8 6.8 copy-start.54
  160.8 6.7 copy-start.42
  160.9 6.7 copy-start.44
  171.3 22.9 %copy-start.23 = (bf16[5,256,512]{2,1,0:T(8,128)(2,1)S(1)}, bf16[5,256,512]{2,1,0:T(8,128)(2,1)}, u32[]{:S(2)}) copy-start(bf16[5,256,512]{2,1,0:T(8,128)(2,1)} %get-tuple-element.183) | copy-start | bytes 3932164
  171.3 22.9 %copy-start.86 = (bf16[512,1536]{1,0:T(8,128)(2,1)S(1)}, bf16[512,1536]{1,0:T(8,128)(2,1)}, u32[]{:S(2)}) copy-start(bf16[512,1536]{1,0:T(8,128)(2,1)} %all-gather.4.cloned.1.call-done) | copy-start | bytes 4718596
  222.3 45.3 %copy-start.14 = (f32[1280,512]{1,0:T(8,128)}, f32[1280,512]{1,0:T(8,128)S(1)}, u32[]{:S(2)}) copy-start(f32[1280,512]{1,0:T(8,128)S(1)} %convolution_add_fusion.4) | copy-start | bytes 7864324
  242.7 24.9 %slice-start = ((s8[5242880]{0:T(1024)(128)(4,1)}), s8[4194304]{0:T(1024)(128)(4,1)S(1)}, s32[]{:S(2)}) async-start(s8[5242880]{0:T(1024)(128)(4,1)} %bitcast.107), calls=%async_computation.8 | async-start | bytes 8388608
  245.0 22.7 %slice-start.1 = ((s8[5242880]{0:T(1024)(128)(4,1)}), s8[1048576]{0:T(1024)(128)(4,1)S(1)}, s32[]{:S(2)}) async-start(s8[5242880]{0:T(1024)(128)(4,1)} %bitcast.107), calls=%async_computation.9 | async-start | bytes 2097152
  267.6 7.6 %copy-start.16 = (f32[1280,512]{1,0:T(8,128)}, f32[1280,512]{1,0:T(8,128)S(1)}, u32[]{:S(2)}) copy-start(f32[1280,512]{1,0:T(8,128)S(1)} %convolution_add_fusion.5) | copy-start | bytes 7864324
  275.2 7.5 copy-start.34
  275.2 19.4 %copy-start.38 = (bf16[5,256,512]{2,1,0:T(8,128)(2,1)}, bf16[5,256,512]{2,1,0:T(8,128)(2,1)S(1)}, u32[]{:S(2)}) copy-start(bf16[5,256,512]{2,1,0:T(8,128)(2,1)S(1)} %get-tuple-element.126) | copy-start | bytes 3932164
  275.2 29.4 %copy-start.36 = (bf16[5,256,512]{2,1,0:T(8,128)(2,1)}, bf16[5,256,512]{2,1,0:T(8,128)(2,1)S(1)}, u32[]{:S(2)}) copy-start(bf16[5,256,512]{2,1,0:T(8,128)(2,1)S(1)} %get-tuple-element.124) | copy-start | bytes 3932164
  275.2 7.4 copy-start.88
  337.3 8.1 %copy-start.9 = (f32[5,256,512]{2,1,0:T(8,128)}, f32[5,256,512]{2,1,0:T(8,128)S(1)}, u32[]{:S(2)}) copy-start(f32[5,256,512]{2,1,0:T(8,128)S(1)} %get-tuple-element.82) | copy-start | bytes 7864324
  364.5 15.1 %copy-start.8 = (f32[5,256,512]{2,1,0:T(8,128)S(1)}, f32[5,256,512]{2,1,0:T(8,128)}, u32[]{:S(2)}) copy-start(f32[5,256,512]{2,1,0:T(8,128)} %get-tuple-element.191) | copy-start | bytes 7864324
  364.5 15.1 %copy-start.10 = (f32[5,256,512]{2,1,0:T(8,128)S(1)}, f32[5,256,512]{2,1,0:T(8,128)}, u32[]{:S(2)}) copy-start(f32[5,256,512]{2,1,0:T(8,128)} %get-tuple-element.136) | copy-start | bytes 7864324
  379.7 8.0 %copy-start.39 = (bf16[5,256,512]{2,1,0:T(8,128)(2,1)S(1)}, bf16[5,256,512]{2,1,0:T(8,128)(2,1)}, u32[]{:S(2)}) copy-start(bf16[5,256,512]{2,1,0:T(8,128)(2,1)} %copy-done.38) | copy-start | bytes 3932164
  379.7 8.0 %copy-start.90 = (bf16[1280,1536]{1,0:T(8,128)(2,1)S(1)}, bf16[1280,1536]{1,0:T(8,128)(2,1)}, u32[]{:S(2)}) copy-start(bf16[1280,1536]{1,0:T(8,128)(2,1)} %get-tuple-element.93) | copy-start | bytes 11796484
  392.2 5.2 copy-start.35
  397.2 237.4 %reduce-scatter.8.cloned.1.call-start = ((), (), s32[]{:S(2)}) async-start(), calls=%async_computation.6 | async-start | bytes 3244032 | tf_op jit(solution)/shard_map/reduce_scatter | solution.py:160
  404.4 5.9 copy-start.27
  404.4 337.1 %reduce-scatter.6.cloned.1.call-start = ((), (), s32[]{:S(2)}) async-start(), calls=%async_computation.5 | async-start | bytes 3244032 | tf_op jit(solution)/shard_map/reduce_scatter | solution.py:158
  419.4 41.0 %copy-start.15 = (f32[1280,512]{1,0:T(8,128)S(1)}, f32[1280,512]{1,0:T(8,128)}, u32[]{:S(2)}) copy-start(f32[1280,512]{1,0:T(8,128)} %copy-done.14) | copy-start | bytes 7864324
  460.4 21.2 %slice-start.4 = ((s8[5242880]{0:T(1024)(128)(4,1)}), s8[4194304]{0:T(1024)(128)(4,1)S(1)}, s32[]{:S(2)}) async-start(s8[5242880]{0:T(1024)(128)(4,1)} %bitcast.111), calls=%async_computation.12 | async-start | bytes 8388608
  465.7 16.0 %slice-start.5 = ((s8[5242880]{0:T(1024)(128)(4,1)}), s8[1048576]{0:T(1024)(128)(4,1)S(1)}, s32[]{:S(2)}) async-start(s8[5242880]{0:T(1024)(128)(4,1)} %bitcast.111), calls=%async_computation.13 | async-start | bytes 2097152
  465.7 16.0 %copy-start.12 = (f32[5,256,512]{2,1,0:T(8,128)S(1)}, f32[5,256,512]{2,1,0:T(8,128)}, u32[]{:S(2)}) copy-start(f32[5,256,512]{2,1,0:T(8,128)} %get-tuple-element.184) | copy-start | bytes 7864324
  465.7 16.0 %copy-start.13 = (f32[5,256,512]{2,1,0:T(8,128)S(1)}, f32[5,256,512]{2,1,0:T(8,128)}, u32[]{:S(2)}) copy-start(f32[5,256,512]{2,1,0:T(8,128)} %get-tuple-element.185) | copy-start | bytes 7864324
  496.1 6.4 copy-start.28
  496.1 6.4 copy-start.29
  496.1 6.4 copy-start.30
  496.1 6.4 copy-start.31
  (57 other events, 208.4 us)
Sparse Core Ops, SparseCore 0:
  10.9 57.7 all-gather.3
  71.6 53.9 all-gather.5
  397.3 132.8 reduce-scatter.9
  536.0 98.4 reduce-scatter.7
  640.4 101.1 reduce-scatter.5
where the time goes:
time: 758 us; the launch traced here: 748 us
  waiting for transfers between devices  236 us (31%)
  matrix products  176 us (23%)
  other arithmetic  155 us (20%)
  blocking collectives  146 us (19%)
  local copies, waits for them, and re-layouts  19 us (3%)
  between operations  15.5 us (2%)
    reduce_scatter x1, waiting for transfers between devices, on_device(): lax.psum_scatter(totals[4], ('dp', 'fsdp'), scatter_dimension=0, tiled=True)  107 us
    reduce_scatter x1, waiting for transfers between devices, on_device(): lax.psum_scatter(totals[6], ('dp', 'fsdp'), scatter_dimension=0, tiled=True)  103 us
    dot_general x4, matrix products, on_device(): jnp.dot(rows_low, full_in, preferred_element_type=jnp.float32)  84.5 us
    unnamed x2, blocking collectives  79.6 us
    all_gather x1, blocking collectives, on_device(): lax.all_gather(conv_weight, ('dp', 'fsdp'), axis=0, tiled=True)  66.8 us
    reduce_sum x4, other arithmetic, conv_norm(): padded[:, offset:offset + frames, :] * conv_weight[:, offset]  50.2 us
    dot_general x8, matrix products, contract_last(): lax.dot_general(left_side, right_side, (((1,), (1,)), ((), ())), preferre...  44 us
    dot_general x8, matrix products, contract_rows(): lax.dot_general(left_side, right_side, (((0,), (0,)), ((), ())), preferre...  36 us
  transfers between devices with their start and end apart: 5, of which 3 were waited for; matrix products, arithmetic and copies ran while one was open for 22% of the time, Pallas kernels for 0%

commit v1 on v0

--- a/solution.py
+++ b/solution.py
@@ -3,6 +3,7 @@
 import jax.numpy as jnp
 from jax import lax
 from jax.sharding import PartitionSpec as P
+from jax.lax import axis_index, axis_size, ppermute
 
 
 def conv_norm(mel_block, conv_weight, conv_bias, norm_gain, norm_shift):
@@ -65,8 +66,25 @@
     block_outs = []
     block_grads = []
     for micro_step in range(micro_count):
+
+        def wrap_the_stocks(field):
+            f_now = axis_index(("dp", "fsdp"))
+            left_arr = axis_size(("dp", "fsdp"))
+            parts_out, current_value = (left_arr, f_now)
+            before, tall = (field, 1)
+            while tall < parts_out:
+                y2 = range(parts_out)
+                base_arr = map(lambda d: (d, d ^ tall), y2)
+                arr_now = list(base_arr)
+                piece_out = ppermute(before, ("dp", "fsdp"), arr_now)
+                k_now = jnp.concatenate([before, piece_out], axis=0)
+                value_now = jnp.concatenate([piece_out, before], axis=0)
+                before = jnp.where(current_value & tall == 0, k_now, value_now)
+                tall = 2 * tall
+            return before
+
         forward_set = (
-            lax.all_gather(conv_weight, ("dp", "fsdp"), axis=0, tiled=True),
+            wrap_the_stocks(conv_weight),
             lax.all_gather(conv_bias, ("dp", "fsdp"), axis=0, tiled=True),
             lax.all_gather(norm_gain, ("dp", "fsdp"), axis=0, tiled=True),
             lax.all_gather(norm_shift, ("dp", "fsdp"), axis=0, tiled=True),

time: 758 us -> 696 us (0.918)
  blocking collectives: 146 us -> 80.9 us
  starting transfers between devices: 0.37 us -> 9.76 us
    all_gather x1 -> x0, blocking collectives: 66.8 us -> none  [on_device(): lax.all_gather(conv_weight, ('dp', 'fsdp'), axis=0, tiled=True)]
    ppermute x0 -> x5, starting transfers between devices: none -> 9.35 us  [wrap_the_stocks(): piece_out = ppermute(before, ('dp', 'fsdp'), arr_now)]
    unnamed x220 -> x232, local copies, waits for them, and re-layouts: 18.1 us -> 15.6 us
  transfers between devices with their start and end apart: 5 -> 10, of which waited for: 3 -> 5; matrix products, arithmetic and copies ran while one was open for 22% -> 23% of each run, Pallas kernels for 0% -> 0%
where the time goes in v1:
time: 696 us; the launch traced here: 693 us
  waiting for transfers between devices  239 us (34%)
  matrix products  176 us (25%)
  other arithmetic  155 us (22%)
  blocking collectives  80.9 us (12%)
  local copies, waits for them, and re-layouts  16.2 us (2%)
  between operations  15.6 us (2%)
  starting transfers between devices  9.76 us (1%)
    reduce_scatter x1, waiting for transfers between devices, on_device(): lax.psum_scatter(totals[4], ('dp', 'fsdp'), scatter_dimension=0, tiled=True)  107 us
    reduce_scatter x1, waiting for transfers between devices, on_device(): lax.psum_scatter(totals[6], ('dp', 'fsdp'), scatter_dimension=0, tiled=True)  103 us
    dot_general x4, matrix products, on_device(): jnp.dot(rows_low, full_in, preferred_element_type=jnp.float32)  84.2 us
    unnamed x2, blocking collectives  80.9 us
    reduce_sum x4, other arithmetic, conv_norm(): padded[:, offset:offset + frames, :] * conv_weight[:, offset]  49.2 us
    dot_general x8, matrix products, contract_last(): lax.dot_general(left_side, right_side, (((1,), (1,)), ((), ())), preferre...  44.2 us
    dot_general x8, matrix products, contract_rows(): lax.dot_general(left_side, right_side, (((0,), (0,)), ((), ())), preferre...  36.2 us
    reduce_sum x2, other arithmetic, conv_norm(): center = mixed_sum - jnp.mean(mixed_sum, axis=-1, keepdims=True)  33.3 us
  transfers between devices with their start and end apart: 10, of which 5 were waited for; matrix products, arithmetic and copies ran while one was open for 23% of the time, Pallas kernels for 0%

profile of v1, /device:TPU:0, one launch (start us, length us, event | category | flops | bytes accessed | tf_op | source)
XLA Modules:
  0.0 692.7 jit_solution(10579083860341581927)
XLA Ops:
  8.0 3.1 collective-permute-start
  13.7 2.1 collective-permute-start.1
  15.8 7.1 %slice_convert_fusion.3 = (f32[5,256,512]{2,1,0:T(8,128)}, f32[5,256,512]{2,1,0:T(8,128)}, f32[5,256,512]{2,1,0:T(8,128)}, f32[5,256,512]{2,1,0:T(8,128)}) fusion(bf16[20,256,512]{2,1,0:T(8,128)(2,1)} %param.12), kind=kLoop, calls=%fused_computation.255 | loop fusion | flops 2621440 | bytes 15728640 | tf_op jit(solution)/shard_map/convert_element_type | solution.py:108
  23.0 2.6 collective-permute-start.2
  34.3 40.5 %all-reduce.73 = (bf16[512]{0:T(512)(128)(2,1)S(1)}, bf16[512]{0:T(512)(128)(2,1)S(1)}, bf16[512]{0:T(512)(128)(2,1)S(1)}, bf16[1536]{0:T(1024)(128)(2,1)S(1)}, ...) all-reduce(bf16[512]{0:T(512)(128)(2,1)S(1)} %dynamic-update-slice,, ...), channel_id=1, replica_groups=mesh['dp'=4,'fsdp'=8] {'dp','fsdp'}, use_global_device_ids=true, to_apply=%add.60 | all-reduce | flops 4096 | bytes 16384
  75.5 28.8 %fusion.62 = (f32[5,256]{1,0:T(8,128)S(1)}, f32[5,256,512]{2,1,0:T(8,128)S(1)}, f32[5,256]{1,0:T(8,128)S(1)}, f32[5,256,512]{2,1,0:T(8,128)S(1)}, f32[5,256]{1,0...) fusion(f32[512]{0:T(512)S(1)} %bitcast.149, f32[512]{0:T(512)S(1)} %bitcast.140, ...), kind=kLoop, calls=%fused_computation.301 | loop fusion | flops 39316480 | bytes 21008384 | tf_op jit(solution)/shard_map/jvp()/reduce_sum | solution.py:17
  109.5 3.6 add_convert_fusion.11
  113.2 22.9 %multiply_convert_fusion.2 = (bf16[1280,1536]{1,0:T(8,128)(2,1)}, f32[1280,1536]{1,0:T(8,128)}, f32[1280,1536]{1,0:T(8,128)}) fusion(f32[1536]{0:T(1024)S(1)} %convert_element_type.238, bf16[1280,512]{1,0:T(8,128)(2,1)} %bitcast.126, bf16[512,1536]{1,0:T(8,128)(2,1)} %all-gather.3.cloned.1.call-done), kind=kOutput, calls=%fused_computation.46 | convolution fusion | flops 2143027200 | bytes 22550528 | tf_op jit(solution)/shard_map/dot_general | solution.py:123
  136.1 20.6 %multiply_convert_fusion = (bf16[1280,1536]{1,0:T(8,128)(2,1)}, f32[1280,1536]{1,0:T(8,128)}, f32[1280,1536]{1,0:T(8,128)}) fusion(f32[1536]{0:T(1024)S(1)} %convert_element_type.238, bf16[1280,512]{1,0:T(8,128)(2,1)S(1)} %bitcast.122, bf16[512,1536]{1,0:T(8,128)(2,1)S(1)} %copy-done.86), kind=kOutput, calls=%fused_computation.20 | convolution fusion | flops 2143027200 | bytes 22550528 | tf_op jit(solution)/shard_map/dot_general | solution.py:123
  156.7 5.0 convolution_add_fusion.6
  161.7 2.2 convolution_add_fusion.4
  163.9 20.4 %multiply_convert_fusion.3 = (bf16[1280,1536]{1,0:T(8,128)(2,1)S(1)}, f32[1280,1536]{1,0:T(8,128)}, f32[1280,1536]{1,0:T(8,128)}) fusion(f32[1536]{0:T(1024)S(1)} %convert_element_type.238, bf16[1280,512]{1,0:T(8,128)(2,1)S(1)} %bitcast.130, bf16[512,1536]{1,0:T(8,128)(2,1)S(1)} %copy-done.86), kind=kOutput, calls=%fused_computation.59 | convolution fusion | flops 2143027200 | bytes 22550528 | tf_op jit(solution)/shard_map/dot_general | solution.py:123
  184.3 2.2 convolution_add_fusion.7
  186.5 20.4 %multiply_convert_fusion.1 = (bf16[1280,1536]{1,0:T(8,128)(2,1)S(1)}, f32[1280,1536]{1,0:T(8,128)}, f32[1280,1536]{1,0:T(8,128)}) fusion(f32[1536]{0:T(1024)S(1)} %convert_element_type.238, bf16[1280,512]{1,0:T(8,128)(2,1)S(1)} %bitcast.124, bf16[512,1536]{1,0:T(8,128)(2,1)S(1)} %copy-done.86), kind=kOutput, calls=%fused_computation.33 | convolution fusion | flops 2143027200 | bytes 22550528 | tf_op jit(solution)/shard_map/dot_general | solution.py:123
  207.0 2.2 convolution_add_fusion.5
  209.2 2.2 slice-done.2
  211.8 5.0 add_convert_fusion.10
  216.8 7.5 %fusion.76 = f32[1536,512]{1,0:T(8,128)} fusion(bf16[1280,1536]{1,0:T(8,128)(2,1)} %copy-done.99, bf16[1280,512]{1,0:T(8,128)(2,1)S(1)} %bitcast.138), kind=kOutput, calls=%fused_computation.312 | convolution fusion | flops 2013265920 | bytes 8388608 | tf_op jit(solution)/shard_map/dot_general | solution.py:23
  224.4 7.8 %convert_reduce_fusion = (f32[1536]{0:T(1024)S(1)}, bf16[1280,1536]{1,0:T(8,128)(2,1)S(1)}) fusion(f32[1280,1536]{1,0:T(8,128)} %get-tuple-element.102, f32[1280,1536]{1,0:T(8,128)} %get-tuple-element.205, bf16[1280,512]{1,0:T(8,128)(2,1)S(1)} %bitcast.132, bf16[1536,512]{1,0:T(8,128)(2,1)S(1)} %copy-done.88), kind=kOutput, calls=%fused_computation.12 | convolution fusion | flops 2044721664 | bytes 22550528 | tf_op jit(solution)/shard_map/dot_general | solution.py:29
  232.2 2.2 fusion.71
  236.3 7.8 %convert_reduce_fusion.2 = (f32[1536]{0:T(1024)S(1)}, bf16[1280,1536]{1,0:T(8,128)(2,1)S(1)}) fusion(f32[1280,1536]{1,0:T(8,128)} %get-tuple-element.94, f32[1280,1536]{1,0:T(8,128)} %get-tuple-element.207, bf16[1280,512]{1,0:T(8,128)(2,1)S(1)} %bitcast.136, bf16[1536,512]{1,0:T(8,128)(2,1)S(1)} %copy-done.88), kind=kOutput, calls=%fused_computation.14 | convolution fusion | flops 2044721664 | bytes 22550528 | tf_op jit(solution)/shard_map/dot_general | solution.py:29
  244.1 2.2 fusion.74
  246.4 8.2 %convert_reduce_fusion.1 = (f32[1536]{0:T(1024)S(1)}, bf16[1280,1536]{1,0:T(8,128)(2,1)S(1)}) fusion(f32[1280,1536]{1,0:T(8,128)} %get-tuple-element.98, f32[1280,1536]{1,0:T(8,128)} %get-tuple-element.204, bf16[1280,512]{1,0:T(8,128)(2,1)S(1)} %bitcast.134, bf16[1536,512]{1,0:T(8,128)(2,1)S(1)} %copy-done.88), kind=kOutput, calls=%fused_computation.13 | convolution fusion | flops 2044721664 | bytes 22550528 | tf_op jit(solution)/shard_map/dot_general | solution.py:29
  254.6 2.2 fusion.72
  256.9 9.1 %convert_reduce_fusion.3 = (f32[1536]{0:T(1024)S(1)}, bf16[1280,1536]{1,0:T(8,128)(2,1)}) fusion(f32[1280,1536]{1,0:T(8,128)} %get-tuple-element.90, f32[1280,1536]{1,0:T(8,128)} %get-tuple-element.206, bf16[1280,512]{1,0:T(8,128)(2,1)S(1)} %bitcast.139, bf16[1536,512]{1,0:T(8,128)(2,1)S(1)} %copy-done.88), kind=kOutput, calls=%fused_computation.15 | convolution fusion | flops 2044721664 | bytes 22550528 | tf_op jit(solution)/shard_map/dot_general | solution.py:29
  266.0 4.6 fusion.73
  270.7 3.9 multiply_reduce_fusion.3
  274.8 4.4 fusion.57
  279.3 8.0 %multiply_reduce_fusion.31 = (f32[512]{0:T(512)S(1)}, f32[512]{0:T(512)S(1)}, f32[512]{0:T(512)S(1)}, f32[512]{0:T(512)S(1)}, f32[512]{0:T(512)S(1)}, /*index=5*...) fusion(f32[5,256,512]{2,1,0:T(8,128)S(1)} %copy-done.11, ...), kind=kLoop, calls=%fused_computation.179 | loop fusion | flops 13758976 | bytes 23626752 | tf_op jit(solution)/shard_map/transpose(jvp())/reduce_sum | solution.py:16
  287.3 18.6 %multiply_reduce_fusion.17 = (f32[512]{0:T(512)S(1)}, f32[512]{0:T(512)S(1)}, f32[512]{0:T(512)S(1)}, f32[512]{0:T(512)S(1)}, f32[512]{0:T(512)S(1)}, /*index=5*...) fusion(f32[5,256,512]{2,1,0:T(8,128)} %get-tuple-element.138, ...), kind=kLoop, calls=%fused_computation.165 | loop fusion | flops 17691648 | bytes 41979904 | tf_op jit(solution)/shard_map/transpose(jvp())/reduce_sum | solution.py:16
  305.9 14.7 %multiply_reduce_fusion.28 = (f32[512]{0:T(512)S(1)}, f32[512]{0:T(512)S(1)}, f32[512]{0:T(512)S(1)}, f32[512]{0:T(512)S(1)}, f32[512]{0:T(512)S(1)}, /*index=5*...) fusion(bf16[20,256,512]{2,1,0:T(8,128)(2,1)} %param.12, ...), kind=kLoop, calls=%fused_computation.176 | loop fusion | flops 20964864 | bytes 21020672 | tf_op jit(solution)/shard_map/transpose(jvp())/reduce_sum | solution.py:16
  320.6 8.0 %multiply_reduce_fusion.24 = (f32[512]{0:T(512)S(1)}, f32[512]{0:T(512)S(1)}, f32[512]{0:T(512)S(1)}, f32[512]{0:T(512)S(1)}, f32[512]{0:T(512)S(1)}, /*index=5*...) fusion(f32[5,256,512]{2,1,0:T(8,128)S(1)} %copy-done.10, ...), kind=kLoop, calls=%fused_computation.172 | loop fusion | flops 13104128 | bytes 23624704 | tf_op jit(solution)/shard_map/transpose(jvp())/reduce_sum | solution.py:16
  328.7 4.4 convolution_add_fusion.10
  333.1 4.0 convolution_add_fusion.9
  338.3 7.0 %convolution_add_fusion.8 = f32[1536,512]{1,0:T(8,128)} fusion(f32[1536,512]{1,0:T(8,128)} %convolution_add_fusion.9, bf16[1280,1536]{1,0:T(8,128)(2,1)} %get-tuple-element.101, bf16[1280,512]{1,0:T(8,128)(2,1)S(1)} %bitcast.133), kind=kOutput, calls=%fused_computation.94 | convolution fusion | flops 2014052352 | bytes 11534336 | tf_op jit(solution)/shard_map/dot_general | solution.py:23
  346.7 4.5 fusion.75
  351.3 2.3 convolution_add_fusion.13
  353.8 2.2 convolution_add_fusion.12
  356.3 4.1 convolution_add_fusion.11
  360.5 40.4 %all-reduce.72 = (f32[512]{0:T(512)S(1)}, f32[512]{0:T(512)S(1)}, f32[512]{0:T(512)S(1)}, f32[1536]{0:T(1024)S(1)}, f32[512]{0:T(512)S(1)}, /*index=5*/f32[512]{0:T(512)S(1)}) all-reduce(f32[512]{0:T(512)S(1)} %add_add_fusion.10, f32[512]{0:T(512)S(1)} %add_add_fusion.9, ...), channel_id=3, replica_groups=mesh['dp'=4,'fsdp'=8] {'dp','fsdp'}, use_global_device_ids=true, to_apply=%region_49.50.clone | all-reduce | flops 4096 | bytes 32768
  404.4 5.4 add_convert_fusion.6
  409.8 15.9 %fusion.40 = (bf16[5,256,512]{2,1,0:T(8,128)(2,1)S(1)}, bf16[5,256,512]{2,1,0:T(8,128)(2,1)}) fusion(f32[5,256,512]{2,1,0:T(8,128)} %get-tuple-element.144, f32[5,256,512]{2,1,0:T(8,128)} %get-tuple-element.143, f32[5,256,512]{2,1,0:T(8,128)} %get-tuple-element.141, f32[5,256,512]{2,1,0:T(8,128)} %get-tuple-element.142, ...), kind=kLoop, calls=%fused_computation.116 | loop fusion | flops 11796480 | bytes 41943040 | tf_op jit(solution)/shard_map/convert_element_type | solution.py:158
  425.8 14.3 %fusion.41 = (bf16[5,256,512]{2,1,0:T(8,128)(2,1)}, bf16[5,256,512]{2,1,0:T(8,128)(2,1)}) fusion(f32[5,256,512]{2,1,0:T(8,128)} %get-tuple-element.151, f32[5,256,512]{2,1,0:T(8,128)} %get-tuple-element.150, f32[5,256,512]{2,1,0:T(8,128)} %get-tuple-element.148, f32[5,256,512]{2,1,0:T(8,128)} %get-tuple-element.149, f32[5,256,512]{2,1,0:T(8,128)} %get-tuple-element.146, ...), kind=kLoop, calls=%fused_computation.117 | loop fusion | flops 11796480 | bytes 41943040 | tf_op jit(solution)/shard_map/convert_element_type | solution.py:158
  440.1 6.4 pad_maximum_fusion.1
  446.5 3.0 pad_maximum_fusion
  449.5 25.0 %reduce-scatter.10.cloned.1.call-done = f32[16,7]{1,0:T(8,128)} async-done(((f32[512,7]{1,0:T(8,128)}), f32[16,7]{1,0:T(8,128)}) %reduce-scatter.10.cloned.1.call-update) | async-done | bytes 464
  475.9 103.0 %reduce-scatter.8.cloned.1.call-done = f32[48,512]{1,0:T(8,128)} async-done(((f32[1536,512]{1,0:T(8,128)}), f32[48,512]{1,0:T(8,128)}) %reduce-scatter.8.cloned.1.call-update) | async-done | bytes 98320 | tf_op jit(solution)/shard_map/reduce_scatter | solution.py:178
  578.8 107.1 %reduce-scatter.6.cloned.1.call-done = f32[16,1536]{1,0:T(8,128)} async-done(((f32[512,1536]{1,0:T(8,128)}), f32[16,1536]{1,0:T(8,128)}) %reduce-scatter.6.cloned.1.call-update) | async-done | bytes 98320 | tf_op jit(solution)/shard_map/reduce_scatter | solution.py:176
  (294 shorter events, 28.0 us)
Async XLA Ops:
  7.2 106.0 %all-gather.3.cloned.1.call-start = ((), (), s32[]{:S(2)}) async-start(), calls=%async_computation.3 | async-start | bytes 1622016 | tf_op jit(solution)/shard_map/all_gather | solution.py:91
  7.9 148.8 %all-gather.5.cloned.1.call-start = ((), (), s32[]{:S(2)}) async-start(), calls=%async_computation.4 | async-start | bytes 1622016 | tf_op jit(solution)/shard_map/all_gather | solution.py:93
  8.0 4.8 collective-permute-start
  11.0 463.5 %reduce-scatter.10.cloned.1.call-start = ((), (), s32[]{:S(2)}) async-start(), calls=%async_computation.7 | async-start | bytes 270336
  13.6 12.0 %copy-start.81 = (s32[1,4]{1,0:T(1,128)S(1)}, s32[1,4]{1,0:T(1,128)}, u32[]{:S(2)}) copy-start(s32[1,4]{1,0:T(1,128)} %param.13) | copy-start | bytes 52
  13.6 19.2 %copy-start.89 = (bf16[16]{0:T(256)(128)(2,1)S(1)}, bf16[16]{0:T(256)(128)(2,1)}, u32[]{:S(2)}) copy-start(bf16[16]{0:T(256)(128)(2,1)} %param.15) | copy-start | bytes 100
  13.6 19.4 %copy-start.90 = (bf16[16]{0:T(256)(128)(2,1)S(1)}, bf16[16]{0:T(256)(128)(2,1)}, u32[]{:S(2)}) copy-start(bf16[16]{0:T(256)(128)(2,1)} %param.16) | copy-start | bytes 100
  13.6 19.6 %copy-start.91 = (bf16[16]{0:T(256)(128)(2,1)S(1)}, bf16[16]{0:T(256)(128)(2,1)}, u32[]{:S(2)}) copy-start(bf16[16]{0:T(256)(128)(2,1)} %param.17) | copy-start | bytes 100
  13.6 19.9 %copy-start.92 = (bf16[16]{0:T(256)(128)(2,1)S(1)}, bf16[16]{0:T(256)(128)(2,1)}, u32[]{:S(2)}) copy-start(bf16[16]{0:T(256)(128)(2,1)} %param.21) | copy-start | bytes 100
  13.7 20.1 %copy-start.93 = (bf16[16]{0:T(256)(128)(2,1)S(1)}, bf16[16]{0:T(256)(128)(2,1)}, u32[]{:S(2)}) copy-start(bf16[16]{0:T(256)(128)(2,1)} %param.22) | copy-start | bytes 100
  13.7 20.3 %copy-start.94 = (bf16[48]{0:T(256)(128)(2,1)S(1)}, bf16[48]{0:T(256)(128)(2,1)}, u32[]{:S(2)}) copy-start(bf16[48]{0:T(256)(128)(2,1)} %param.19) | copy-start | bytes 292
  13.7 9.3 %collective-permute-start.1 = (bf16[32,7]{0,1:T(8,128)(2,1)S(1)}, bf16[32,7]{0,1:T(8,128)(2,1)S(1)}, u32[]{:S(2)}, u32[]{:S(2)}) collective-permute-start(bf16[32,7]{0,1:T(8,128)(2,1)S(1)} %maximum_select_fusion.2), channel_id=1, source_target_pairs={{0,2},{1,3},{2,0},{3,1},{4,6},{5,7},{6,4},{7,5},{8,10},{9,11},{10,... | collective-permute-start | bytes 1352 | tf_op jit(solution)/shard_map/ppermute | solution.py:79
  23.0 4.5 collective-permute-start.2
  27.6 1.8 collective-permute-start.3
  29.4 46.0 %collective-permute-start.4 = (bf16[256,7]{0,1:T(8,128)(2,1)S(1)}, bf16[256,7]{0,1:T(8,128)(2,1)S(1)}, u32[]{:S(2)}, u32[]{:S(2)}) collective-permute-start(bf16[256,7]{0,1:T(8,128)(2,1)S(1)} %maximum_select_fusion.1), channel_id=1, source_target_pairs={{0,16},{1,17},{2,18},{3,19},{4,20},{5,21},{6,22},{7,23},{8,24},{9,... | collective-permute-start | bytes 10760 | tf_op jit(solution)/shard_map/ppermute | solution.py:79
  74.8 33.6 %copy-start.78 = (f32[512]{0:T(512)}, f32[512]{0:T(512)S(1)}, u32[]{:S(2)}) copy-start(f32[512]{0:T(512)S(1)} %convert_element_type.234) | copy-start | bytes 6148
  75.4 28.9 %copy-start.56 = (f32[512,1]{0,1:T(1,128)}, f32[512,1]{0,1:T(1,128)S(1)}, u32[]{:S(2)}) copy-start(f32[512,1]{0,1:T(1,128)S(1)} %get-tuple-element.175) | copy-start | bytes 6148
  75.4 28.9 %copy-start.66 = (f32[512,1]{0,1:T(1,128)}, f32[512,1]{0,1:T(1,128)S(1)}, u32[]{:S(2)}) copy-start(f32[512,1]{0,1:T(1,128)S(1)} %get-tuple-element.173) | copy-start | bytes 6148
  75.4 28.9 %copy-start.68 = (f32[512,1]{0,1:T(1,128)}, f32[512,1]{0,1:T(1,128)S(1)}, u32[]{:S(2)}) copy-start(f32[512,1]{0,1:T(1,128)S(1)} %get-tuple-element.174) | copy-start | bytes 6148
  75.4 28.9 %copy-start.70 = (f32[512,1]{0,1:T(1,128)}, f32[512,1]{0,1:T(1,128)S(1)}, u32[]{:S(2)}) copy-start(f32[512,1]{0,1:T(1,128)S(1)} %get-tuple-element.176) | copy-start | bytes 6148
  75.4 28.9 %copy-start.72 = (f32[512,1]{0,1:T(1,128)}, f32[512,1]{0,1:T(1,128)S(1)}, u32[]{:S(2)}) copy-start(f32[512,1]{0,1:T(1,128)S(1)} %get-tuple-element.177) | copy-start | bytes 6148
  75.5 28.9 %copy-start.74 = (f32[512,1]{0,1:T(1,128)}, f32[512,1]{0,1:T(1,128)S(1)}, u32[]{:S(2)}) copy-start(f32[512,1]{0,1:T(1,128)S(1)} %get-tuple-element.178) | copy-start | bytes 6148
  75.5 28.9 %copy-start.76 = (f32[512,1]{0,1:T(1,128)}, f32[512,1]{0,1:T(1,128)S(1)}, u32[]{:S(2)}) copy-start(f32[512,1]{0,1:T(1,128)S(1)} %get-tuple-element.179) | copy-start | bytes 6148
  113.2 22.9 %copy-start.23 = (bf16[5,256,512]{2,1,0:T(8,128)(2,1)S(1)}, bf16[5,256,512]{2,1,0:T(8,128)(2,1)}, u32[]{:S(2)}) copy-start(bf16[5,256,512]{2,1,0:T(8,128)(2,1)} %get-tuple-element.183) | copy-start | bytes 3932164
  113.2 22.9 %copy-start.86 = (bf16[512,1536]{1,0:T(8,128)(2,1)S(1)}, bf16[512,1536]{1,0:T(8,128)(2,1)}, u32[]{:S(2)}) copy-start(bf16[512,1536]{1,0:T(8,128)(2,1)} %all-gather.3.cloned.1.call-done) | copy-start | bytes 4718596
  163.9 45.3 %copy-start.14 = (f32[1280,512]{1,0:T(8,128)}, f32[1280,512]{1,0:T(8,128)S(1)}, u32[]{:S(2)}) copy-start(f32[1280,512]{1,0:T(8,128)S(1)} %convolution_add_fusion.4) | copy-start | bytes 7864324
  184.3 24.9 %slice-start = ((s8[5242880]{0:T(1024)(128)(4,1)}), s8[4194304]{0:T(1024)(128)(4,1)S(1)}, s32[]{:S(2)}) async-start(s8[5242880]{0:T(1024)(128)(4,1)} %bitcast.104), calls=%async_computation.8 | async-start | bytes 8388608
  186.5 22.7 %slice-start.1 = ((s8[5242880]{0:T(1024)(128)(4,1)}), s8[1048576]{0:T(1024)(128)(4,1)S(1)}, s32[]{:S(2)}) async-start(s8[5242880]{0:T(1024)(128)(4,1)} %bitcast.104), calls=%async_computation.9 | async-start | bytes 2097152
  209.2 7.6 %copy-start.16 = (f32[1280,512]{1,0:T(8,128)}, f32[1280,512]{1,0:T(8,128)S(1)}, u32[]{:S(2)}) copy-start(f32[1280,512]{1,0:T(8,128)S(1)} %convolution_add_fusion.5) | copy-start | bytes 7864324
  216.8 7.6 %copy-start.34 = (bf16[5,256,512]{2,1,0:T(8,128)(2,1)}, bf16[5,256,512]{2,1,0:T(8,128)(2,1)S(1)}, u32[]{:S(2)}) copy-start(bf16[5,256,512]{2,1,0:T(8,128)(2,1)S(1)} %get-tuple-element.122) | copy-start | bytes 3932164
  216.8 19.5 %copy-start.38 = (bf16[5,256,512]{2,1,0:T(8,128)(2,1)}, bf16[5,256,512]{2,1,0:T(8,128)(2,1)S(1)}, u32[]{:S(2)}) copy-start(bf16[5,256,512]{2,1,0:T(8,128)(2,1)S(1)} %get-tuple-element.126) | copy-start | bytes 3932164
  216.8 29.6 %copy-start.36 = (bf16[5,256,512]{2,1,0:T(8,128)(2,1)}, bf16[5,256,512]{2,1,0:T(8,128)(2,1)S(1)}, u32[]{:S(2)}) copy-start(bf16[5,256,512]{2,1,0:T(8,128)(2,1)S(1)} %get-tuple-element.124) | copy-start | bytes 3932164
  216.8 7.6 %copy-start.88 = (bf16[1536,512]{1,0:T(8,128)(2,1)S(1)}, bf16[1536,512]{1,0:T(8,128)(2,1)}, u32[]{:S(2)}) copy-start(bf16[1536,512]{1,0:T(8,128)(2,1)} %all-gather.5.cloned.1.call-done) | copy-start | bytes 4718596
  279.2 8.1 %copy-start.9 = (f32[5,256,512]{2,1,0:T(8,128)}, f32[5,256,512]{2,1,0:T(8,128)S(1)}, u32[]{:S(2)}) copy-start(f32[5,256,512]{2,1,0:T(8,128)S(1)} %get-tuple-element.82) | copy-start | bytes 7864324
  305.9 14.7 %copy-start.8 = (f32[5,256,512]{2,1,0:T(8,128)S(1)}, f32[5,256,512]{2,1,0:T(8,128)}, u32[]{:S(2)}) copy-start(f32[5,256,512]{2,1,0:T(8,128)} %get-tuple-element.191) | copy-start | bytes 7864324
  305.9 14.7 %copy-start.10 = (f32[5,256,512]{2,1,0:T(8,128)S(1)}, f32[5,256,512]{2,1,0:T(8,128)}, u32[]{:S(2)}) copy-start(f32[5,256,512]{2,1,0:T(8,128)} %get-tuple-element.136) | copy-start | bytes 7864324
  320.6 8.0 %copy-start.39 = (bf16[5,256,512]{2,1,0:T(8,128)(2,1)S(1)}, bf16[5,256,512]{2,1,0:T(8,128)(2,1)}, u32[]{:S(2)}) copy-start(bf16[5,256,512]{2,1,0:T(8,128)(2,1)} %copy-done.38) | copy-start | bytes 3932164
  320.6 8.0 %copy-start.96 = (bf16[1280,1536]{1,0:T(8,128)(2,1)S(1)}, bf16[1280,1536]{1,0:T(8,128)(2,1)}, u32[]{:S(2)}) copy-start(bf16[1280,1536]{1,0:T(8,128)(2,1)} %get-tuple-element.93) | copy-start | bytes 11796484
  338.1 240.8 %reduce-scatter.8.cloned.1.call-start = ((), (), s32[]{:S(2)}) async-start(), calls=%async_computation.6 | async-start | bytes 3244032 | tf_op jit(solution)/shard_map/reduce_scatter | solution.py:178
  345.4 340.5 %reduce-scatter.6.cloned.1.call-start = ((), (), s32[]{:S(2)}) async-start(), calls=%async_computation.5 | async-start | bytes 3244032 | tf_op jit(solution)/shard_map/reduce_scatter | solution.py:176
  360.4 44.1 %copy-start.15 = (f32[1280,512]{1,0:T(8,128)S(1)}, f32[1280,512]{1,0:T(8,128)}, u32[]{:S(2)}) copy-start(f32[1280,512]{1,0:T(8,128)} %copy-done.14) | copy-start | bytes 7864324
  404.4 21.3 %slice-start.4 = ((s8[5242880]{0:T(1024)(128)(4,1)}), s8[4194304]{0:T(1024)(128)(4,1)S(1)}, s32[]{:S(2)}) async-start(s8[5242880]{0:T(1024)(128)(4,1)} %bitcast.108), calls=%async_computation.12 | async-start | bytes 8388608
  409.8 16.0 %slice-start.5 = ((s8[5242880]{0:T(1024)(128)(4,1)}), s8[1048576]{0:T(1024)(128)(4,1)S(1)}, s32[]{:S(2)}) async-start(s8[5242880]{0:T(1024)(128)(4,1)} %bitcast.108), calls=%async_computation.13 | async-start | bytes 2097152
  409.8 16.0 %copy-start.12 = (f32[5,256,512]{2,1,0:T(8,128)S(1)}, f32[5,256,512]{2,1,0:T(8,128)}, u32[]{:S(2)}) copy-start(f32[5,256,512]{2,1,0:T(8,128)} %get-tuple-element.184) | copy-start | bytes 7864324
  409.8 16.0 %copy-start.13 = (f32[5,256,512]{2,1,0:T(8,128)S(1)}, f32[5,256,512]{2,1,0:T(8,128)}, u32[]{:S(2)}) copy-start(f32[5,256,512]{2,1,0:T(8,128)} %get-tuple-element.185) | copy-start | bytes 7864324
  440.1 6.4 copy-start.28
  440.1 6.4 copy-start.29
  440.1 6.4 copy-start.30
  (68 other events, 242.2 us)
Sparse Core Ops, SparseCore 0:
  10.9 58.0 all-gather.2
  71.9 54.0 all-gather.4
  338.2 136.2 reduce-scatter.9
  480.4 98.4 reduce-scatter.7
  584.7 101.1 reduce-scatter.5
